TPU v7x, 512 devices: a whole 4x8x8 slice. The times are simulated.
512 devices in a mesh: band: 8 (over z_lo, core), dom: 64 (over x, y, z_hi).
Axes of the slice: x: 4, y: 8, z: 8 (z_hi: 2, z_lo: 4; z = z_hi * 4 + z_lo), core: 2. Of those that a mesh axis runs over, the one named last changes fastest.
Arguments:
- orbitals: float32 [96, 128, 128, 128], P('band', 'dom'), may hold values from -6 to 6
- occupations: float32 [96], replicated, may hold values from 0.25 to 2
Outputs:
- exchange_terms: float32 [96, 128, 128, 128], P('band', 'dom')
All inputs are finite; a program needn't handle non-finite values.
Results may differ from a plain program's by a relative error of at most 0.0001.
Values sent between devices are 32-bit elements; how exact they have to be, the bound alone decides.
A program may use at most 128 MiB of HBM per device.

v0:
```python
import jax
import jax.numpy as jnp
from jax import lax
from jax.sharding import PartitionSpec as P

BLOCK = 2
STEPS = 2
SWEEPS = 2


def from_root(block, axis, source):
    block = jnp.where(lax.axis_index(axis) == source, block, jnp.zeros_like(block))
    return lax.psum(block, axis)


def extended(cells, sides, width):
    for axis, dim in sides:
        count = lax.axis_size(axis)
        ends = count - 1
        head = lax.slice_in_dim(cells, 0, width, axis=dim)
        tail = lax.slice_in_dim(cells, cells.shape[dim] - width, cells.shape[dim], axis=dim)
        cells = jnp.concatenate(
            [
                lax.ppermute(tail, axis, [(i, (i + 1) % count) for i in range(ends)]),
                cells,
                lax.ppermute(head, axis, [((i + 1) % count, i) for i in range(ends)]),
            ],
            axis=dim,
        )
    return cells


def lateral(field):
    padded = jnp.pad(field, ((0, 0), (0, 0), (1, 1), (1, 1)))
    total = padded[:, :, 2:, 1:-1] + padded[:, :, :-2, 1:-1]
    return total + padded[:, :, 1:-1, 2:] + padded[:, :, 1:-1, :-2]


def per_device(orbitals, occupations):
    orb_count, planes, cells_y, cells_z = orbitals.shape
    groups = lax.axis_size("band")
    exchange_terms = jnp.zeros(orbitals.shape, jnp.float32)
    for step_index in range(STEPS):
        owner = step_index * (groups // STEPS)
        first = owner * orb_count + step_index * BLOCK
        mine = orbitals[step_index * BLOCK : (step_index + 1) * BLOCK]
        owner_block = from_root(mine, "band", owner)
        weights = occupations[first : first + BLOCK]
        density = (owner_block[:, None] * orbitals[None]).reshape(
            BLOCK * orb_count, planes, cells_y, cells_z
        )
        potential = density / 6.0
        for sweep_index in range(SWEEPS):
            padded = extended(potential, (("dom", 1),), 1)
            along_x = padded[:, 2:] + padded[:, :-2]
            potential = (density + along_x + lateral(potential)) / 6.0
        potential = potential.reshape(BLOCK, orb_count, planes, cells_y, cells_z)
        step_sum = jnp.zeros(orbitals.shape, jnp.float32)
        for block_index in range(BLOCK):
            step_sum = (
                step_sum
                - weights[block_index] * potential[block_index] * owner_block[block_index][None]
            )
        exchange_terms = exchange_terms + step_sum
    return exchange_terms


def solution(mesh):
    in_specs = (P("band", "dom", None, None), P())
    out_specs = P("band", "dom", None, None)
    return jax.shard_map(
        per_device, mesh=mesh, in_specs=in_specs, out_specs=out_specs, check_vma=False
    )
```

profile of v0, /device:TPU:58, one launch (start us, length us, event | category | flops | bytes accessed | tf_op | source)
XLA Modules:
  0.0 701.8 jit_solution(2163669091845171752)
XLA Ops:
  6.5 0.0 all-reduce.7.cloned.1.call-start
  6.5 1.8 slice_select_fusion.1
  8.4 0.0 all-reduce.7.cloned.1.call-update
  8.4 83.7 %all-reduce.7.cloned.1.call-done = (f32[2,2,128,128]{3,2,1,0:T(8,128)}, f32[2,2,128,128]{3,2,1,0:T(8,128)}) async-done(((f32[2,2,128,128]{3,2,1,0:T(8,128)}, f32[2,2,128,128]{3,2,1,0:T(8,128)}), (f32[2,2,128,128]{3,2,1,0:T(8,128)}, f32[2,2,128,128]{3,2,1,0:T(8,128)})) %all-reduce.7.cloned.1.call-update) | async-done | bytes 524304 | tf_op jit(solution)/shard_map/psum | solution.py:13
  92.1 2.3 broadcast_multiply_fusion.1
  94.3 1.2 bitcast_multiply_fusion
  95.6 0.3 fusion.38
  96.0 6.4 collective-permute-start
  102.3 3.4 collective-permute-start.1
  105.7 0.3 fusion.40
  106.1 7.3 %collective-permute-start.4 = (f32[24,1,128,128]{3,2,1,0:T(8,128)S(1)}, f32[24,1,128,128]{3,2,1,0:T(8,128)S(1)}, u32[]{:S(2)}, u32[]{:S(2)}) collective-permute-start(f32[24,1,128,128]{3,2,1,0:T(8,128)S(1)} %get-tuple-element.13), channel_id=1, source_target_pairs={{1,0},{2,1},{3,2},{4,3},{5,4},{6,5},{7,6},{8,7},{9,8},{10,9},{11,1... | collective-permute-start | bytes 4718600 | tf_op jit(solution)/shard_map/ppermute | solution.py:26
  113.3 3.2 collective-permute-start.5
  116.5 215.8 %collective-permute-done = f32[24,1,128,128]{3,2,1,0:T(8,128)S(1)} collective-permute-done((f32[24,1,128,128]{3,2,1,0:T(8,128)S(1)}, f32[24,1,128,128]{3,2,1,0:T(8,128)S(1)}, u32[]{:S(2)}, u32[]{:S(2)}) %collective-permute-start) | collective-permute-done | bytes 1572896 | tf_op jit(solution)/shard_map/ppermute | solution.py:26
  332.3 175.8 %collective-permute-done.1 = f32[24,1,128,128]{3,2,1,0:T(8,128)S(1)} collective-permute-done((f32[24,1,128,128]{3,2,1,0:T(8,128)S(1)}, f32[24,1,128,128]{3,2,1,0:T(8,128)S(1)}, u32[]{:S(2)}, u32[]{:S(2)}) %collective-permute-start.1) | collective-permute-done | bytes 1572896 | tf_op jit(solution)/shard_map/ppermute | solution.py:24
  508.1 2.2 fusion.4
  510.3 0.3 fusion.37
  510.7 1.9 collective-permute-start.2
  512.6 8.4 %collective-permute-start.3 = (f32[24,1,128,128]{3,2,1,0:T(8,128)S(1)}, f32[24,1,128,128]{3,2,1,0:T(8,128)S(1)}, u32[]{:S(2)}, u32[]{:S(2)}) collective-permute-start(f32[24,1,128,128]{3,2,1,0:T(8,128)S(1)} %get-tuple-element.8), channel_id=1, source_target_pairs={{0,1},{1,2},{2,3},{3,4},{4,5},{5,6},{6,7},{7,8},{8,9},{9,10},{10,1... | collective-permute-start | bytes 4718600 | tf_op jit(solution)/shard_map/ppermute | solution.py:24
  521.0 0.0 collective-permute-done.4
  521.0 82.3 %collective-permute-done.5 = f32[24,1,128,128]{3,2,1,0:T(8,128)S(1)} collective-permute-done((f32[24,1,128,128]{3,2,1,0:T(8,128)S(1)}, f32[24,1,128,128]{3,2,1,0:T(8,128)S(1)}, u32[]{:S(2)}, u32[]{:S(2)}) %collective-permute-start.5) | collective-permute-done | bytes 1572896 | tf_op jit(solution)/shard_map/ppermute | solution.py:24
  603.3 2.2 fusion.14
  605.5 0.0 copy-start.2
  605.5 0.0 copy-start
  605.5 0.0 copy-start.1
  605.5 0.3 fusion.39
  605.9 1.9 collective-permute-start.6
  607.8 10.7 %collective-permute-start.7 = (f32[24,1,128,128]{3,2,1,0:T(8,128)S(1)}, f32[24,1,128,128]{3,2,1,0:T(8,128)S(1)}, u32[]{:S(2)}, u32[]{:S(2)}) collective-permute-start(f32[24,1,128,128]{3,2,1,0:T(8,128)S(1)} %get-tuple-element.12), channel_id=1, source_target_pairs={{0,1},{1,2},{2,3},{3,4},{4,5},{5,6},{6,7},{7,8},{8,9},{9,10},{10,1... | collective-permute-start | bytes 4718600 | tf_op jit(solution)/shard_map/ppermute | solution.py:24
  618.5 0.0 copy-done.2
  618.5 0.7 fusion.41
  619.2 0.0 copy-done
  619.2 0.0 copy-done.1
  619.2 36.1 %collective-permute-done.2 = f32[24,1,128,128]{3,2,1,0:T(8,128)S(1)} collective-permute-done((f32[24,1,128,128]{3,2,1,0:T(8,128)S(1)}, f32[24,1,128,128]{3,2,1,0:T(8,128)S(1)}, u32[]{:S(2)}, u32[]{:S(2)}) %collective-permute-start.2) | collective-permute-done | bytes 1572896 | tf_op jit(solution)/shard_map/ppermute | solution.py:26
  655.4 0.0 collective-permute-done.3
  655.4 2.2 fusion.9
  657.6 30.7 %collective-permute-done.6 = f32[24,1,128,128]{3,2,1,0:T(8,128)S(1)} collective-permute-done((f32[24,1,128,128]{3,2,1,0:T(8,128)S(1)}, f32[24,1,128,128]{3,2,1,0:T(8,128)S(1)}, u32[]{:S(2)}, u32[]{:S(2)}) %collective-permute-start.6) | collective-permute-done | bytes 1572896 | tf_op jit(solution)/shard_map/ppermute | solution.py:26
  688.3 0.0 collective-permute-done.7
  688.3 2.2 fusion.19
  690.5 4.5 fusion.30
  (1 shorter events, 0.0 us)
Async XLA Ops:
  6.5 85.5 %all-reduce.7.cloned.1.call-start = ((), (), s32[]{:S(2)}) async-start(), calls=%async_computation | async-start | bytes 1048576 | tf_op jit(solution)/shard_map/psum | solution.py:13
  96.0 236.3 %collective-permute-start = (f32[24,1,128,128]{3,2,1,0:T(8,128)S(1)}, f32[24,1,128,128]{3,2,1,0:T(8,128)S(1)}, u32[]{:S(2)}, u32[]{:S(2)}) collective-permute-start(f32[24,1,128,128]{3,2,1,0:T(8,128)S(1)} %get-tuple-element.9), channel_id=1, source_target_pairs={{1,0},{2,1},{3,2},{4,3},{5,4},{6,5},{7,6},{8,7},{9,8},{10,9},{11,1... | collective-permute-start | bytes 4718600 | tf_op jit(solution)/shard_map/ppermute | solution.py:26
  102.3 405.8 %collective-permute-start.1 = (f32[24,1,128,128]{3,2,1,0:T(8,128)S(1)}, f32[24,1,128,128]{3,2,1,0:T(8,128)S(1)}, u32[]{:S(2)}, u32[]{:S(2)}) collective-permute-start(f32[24,1,128,128]{3,2,1,0:T(8,128)S(1)} %get-tuple-element.10), channel_id=1, source_target_pairs={{0,1},{1,2},{2,3},{3,4},{4,5},{5,6},{6,7},{7,8},{8,9},{9,10},{10,1... | collective-permute-start | bytes 4718600 | tf_op jit(solution)/shard_map/ppermute | solution.py:24
  106.1 414.9 %collective-permute-start.4 = (f32[24,1,128,128]{3,2,1,0:T(8,128)S(1)}, f32[24,1,128,128]{3,2,1,0:T(8,128)S(1)}, u32[]{:S(2)}, u32[]{:S(2)}) collective-permute-start(f32[24,1,128,128]{3,2,1,0:T(8,128)S(1)} %get-tuple-element.13), channel_id=1, source_target_pairs={{1,0},{2,1},{3,2},{4,3},{5,4},{6,5},{7,6},{8,7},{9,8},{10,9},{11,1... | collective-permute-start | bytes 4718600 | tf_op jit(solution)/shard_map/ppermute | solution.py:26
  113.3 490.0 %collective-permute-start.5 = (f32[24,1,128,128]{3,2,1,0:T(8,128)S(1)}, f32[24,1,128,128]{3,2,1,0:T(8,128)S(1)}, u32[]{:S(2)}, u32[]{:S(2)}) collective-permute-start(f32[24,1,128,128]{3,2,1,0:T(8,128)S(1)} %get-tuple-element.14), channel_id=1, source_target_pairs={{0,1},{1,2},{2,3},{3,4},{4,5},{5,6},{6,7},{7,8},{8,9},{9,10},{10,1... | collective-permute-start | bytes 4718600 | tf_op jit(solution)/shard_map/ppermute | solution.py:24
  510.7 144.7 %collective-permute-start.2 = (f32[24,1,128,128]{3,2,1,0:T(8,128)S(1)}, f32[24,1,128,128]{3,2,1,0:T(8,128)S(1)}, u32[]{:S(2)}, u32[]{:S(2)}) collective-permute-start(f32[24,1,128,128]{3,2,1,0:T(8,128)S(1)} %get-tuple-element.7), channel_id=1, source_target_pairs={{1,0},{2,1},{3,2},{4,3},{5,4},{6,5},{7,6},{8,7},{9,8},{10,9},{11,1... | collective-permute-start | bytes 4718600 | tf_op jit(solution)/shard_map/ppermute | solution.py:26
  512.6 142.8 %collective-permute-start.3 = (f32[24,1,128,128]{3,2,1,0:T(8,128)S(1)}, f32[24,1,128,128]{3,2,1,0:T(8,128)S(1)}, u32[]{:S(2)}, u32[]{:S(2)}) collective-permute-start(f32[24,1,128,128]{3,2,1,0:T(8,128)S(1)} %get-tuple-element.8), channel_id=1, source_target_pairs={{0,1},{1,2},{2,3},{3,4},{4,5},{5,6},{6,7},{7,8},{8,9},{9,10},{10,1... | collective-permute-start | bytes 4718600 | tf_op jit(solution)/shard_map/ppermute | solution.py:24
  605.5 13.0 %copy-start.2 = (f32[96]{0:T(128)S(1)}, f32[96]{0:T(128)}, u32[]{:S(2)}) copy-start(f32[96]{0:T(128)} %param.3) | copy-start | bytes 1156
  605.5 13.6 %copy-start = (f32[2,2,128,128]{3,2,1,0:T(8,128)S(1)}, f32[2,2,128,128]{3,2,1,0:T(8,128)}, u32[]{:S(2)}) copy-start(f32[2,2,128,128]{3,2,1,0:T(8,128)} %get-tuple-element.5) | copy-start | bytes 786436
  605.5 13.6 %copy-start.1 = (f32[2,2,128,128]{3,2,1,0:T(8,128)S(1)}, f32[2,2,128,128]{3,2,1,0:T(8,128)}, u32[]{:S(2)}) copy-start(f32[2,2,128,128]{3,2,1,0:T(8,128)} %get-tuple-element.6) | copy-start | bytes 786436
  605.9 82.4 %collective-permute-start.6 = (f32[24,1,128,128]{3,2,1,0:T(8,128)S(1)}, f32[24,1,128,128]{3,2,1,0:T(8,128)S(1)}, u32[]{:S(2)}, u32[]{:S(2)}) collective-permute-start(f32[24,1,128,128]{3,2,1,0:T(8,128)S(1)} %get-tuple-element.11), channel_id=1, source_target_pairs={{1,0},{2,1},{3,2},{4,3},{5,4},{6,5},{7,6},{8,7},{9,8},{10,9},{11,1... | collective-permute-start | bytes 4718600 | tf_op jit(solution)/shard_map/ppermute | solution.py:26
  607.8 80.4 %collective-permute-start.7 = (f32[24,1,128,128]{3,2,1,0:T(8,128)S(1)}, f32[24,1,128,128]{3,2,1,0:T(8,128)S(1)}, u32[]{:S(2)}, u32[]{:S(2)}) collective-permute-start(f32[24,1,128,128]{3,2,1,0:T(8,128)S(1)} %get-tuple-element.12), channel_id=1, source_target_pairs={{0,1},{1,2},{2,3},{3,4},{4,5},{5,6},{6,7},{7,8},{8,9},{9,10},{10,1... | collective-permute-start | bytes 4718600 | tf_op jit(solution)/shard_map/ppermute | solution.py:24
Sparse Core Ops, SparseCore 0:
  10.3 81.7 all-reduce.6
where the time goes:
time: 702 us
  waiting for transfers between devices  624 us (89%)
  starting transfers between devices  43 us (6%)
  other arithmetic  18.7 us (3%)
  between operations  13.6 us (2%)
    ppermute x4, waiting for transfers between devices, extended(): lax.ppermute(head, axis, [((i + 1) % count, i) for i in range(ends)])  283 us
    ppermute x4, waiting for transfers between devices, extended(): lax.ppermute(tail, axis, [(i, (i + 1) % count) for i in range(ends)])  258 us
    psum x1, waiting for transfers between devices, from_root(): return lax.psum(block, axis)  83.7 us
    ppermute x4, starting transfers between devices, extended(): lax.ppermute(tail, axis, [(i, (i + 1) % count) for i in range(ends)])  25.6 us
    ppermute x4, starting transfers between devices, extended(): lax.ppermute(head, axis, [((i + 1) % count, i) for i in range(ends)])  17.5 us
  transfers between devices with their start and end apart: 9, of which 6 were waited for; matrix products, arithmetic and copies ran while one was open for 1% of the time, Pallas kernels for 0%

commit v1 on v0

v1 whole, which is shorter than its diff:
```python
import functools

import jax
import jax.numpy as jnp
from jax import lax
from jax.experimental import pallas as pl
from jax.experimental.pallas import tpu as pltpu
from jax.sharding import PartitionSpec as P

MESH = pl.DeviceIdType.MESH

BLOCK = 2
STEPS = 2
NB = BLOCK * STEPS
CY = 128
CZ = 128
SLAB = 2 * CY
PAIRS = 32
HALF = 6
STRIP = 8

PLANE_OFFSETS = [
    (dx, dy) for dx in range(-2, 3) for dy in range(-2, 3) if abs(dx) + abs(dy) <= 2
]
OFFSETS = [
    (dx, dy, dz)
    for dx, dy in PLANE_OFFSETS
    for dz in range(-2, 3)
    if abs(dx) + abs(dy) + abs(dz) <= 2
]
INDEX = {offset: k for k, offset in enumerate(OFFSETS)}


def coefficient(offset):
    steps = sum(abs(d) for d in offset)
    if steps == 1:
        return 1.0 / 36.0
    return (1.0 if 2 in map(abs, offset) else 2.0) / 216.0


def kernel(
    weight_rows,
    occ_ref,
    x_ref,
    o_ref,
    w_ref,
    block_ref,
    k_ref,
    out_ref,
    own_sem,
    cross_send,
    cross_recv,
    direct_send,
    direct_recv,
    pass_send,
    pass_recv,
    back_send,
    back_recv,
    keep_sem,
    root_send,
    root_recv,
    root_own,
    side_send,
    side_recv,
    core_send,
    core_recv,
):
    band, dom = lax.axis_index("band"), lax.axis_index("dom")
    core, z_lo = lax.rem(band, 2), band // 2
    half, pair = lax.rem(dom, 2), dom // 2
    right_pair = lax.rem(pair + 1, PAIRS)
    left_pair = lax.rem(pair + PAIRS - 1, PAIRS)
    partner = (band, dom + 1 - 2 * half)
    sibling = (band + 1 - 2 * core, dom)
    right = (band, 2 * right_pair + half)
    left = (band, 2 * left_pair + half)
    ahead = (band, 2 * jnp.where(half == 0, right_pair, left_pair) + half)
    behind = (band, 2 * jnp.where(half == 0, left_pair, right_pair) + half)
    first_root = band == 0
    second_root = band == 4

    def rows(slab):
        return pl.ds(pl.multiple_of(slab * SLAB, SLAB), SLAB)

    def remote(src, dst, send, recv, device):
        return pltpu.make_async_remote_copy(
            src_ref=src,
            dst_ref=dst,
            send_sem=send,
            recv_sem=recv,
            device_id=device,
            device_id_type=MESH,
        )

    def own(i):
        return pltpu.make_async_copy(
            x_ref.at[HALF * half + i], w_ref.at[i, rows(1 + half)], own_sem.at[i]
        )

    def cross(i):
        return remote(
            x_ref.at[HALF * (1 - half) + i],
            w_ref.at[i, rows(1 + half)],
            cross_send.at[i],
            cross_recv.at[i],
            partner,
        )

    def direct(i):
        return remote(
            x_ref.at[HALF * half + i],
            w_ref.at[i, rows(3 - 3 * half)],
            direct_send.at[i],
            direct_recv.at[i],
            behind,
        )

    def passed(i):
        return remote(
            w_ref.at[i, rows(2 - half)],
            w_ref.at[i, rows(3 * half)],
            pass_send.at[i],
            pass_recv.at[i],
            ahead,
        )

    def back(i):
        return remote(
            out_ref.at[i, rows(1 - half)],
            o_ref.at[HALF * half + i],
            back_send.at[i],
            back_recv.at[i],
            partner,
        )

    def keep(i):
        return pltpu.make_async_copy(
            out_ref.at[i, rows(half)], o_ref.at[HALF * half + i], keep_sem.at[i]
        )

    def root(group, t, device):
        return remote(
            x_ref.at[pl.ds(BLOCK * group, BLOCK)],
            block_ref.at[pl.ds(BLOCK * group, BLOCK), rows(1 + half)],
            root_send.at[t],
            root_recv.at[half],
            device,
        )

    def root_arrival(slab):
        return remote(
            x_ref.at[pl.ds(BLOCK * core, BLOCK)],
            block_ref.at[pl.ds(BLOCK * core, BLOCK), rows(1 + slab)],
            root_send.at[0],
            root_recv.at[slab],
            sibling,
        )

    def root_local():
        return pltpu.make_async_copy(
            x_ref.at[pl.ds(0, BLOCK)],
            block_ref.at[pl.ds(0, BLOCK), rows(1 + half)],
            root_own,
        )

    mine = pl.ds(BLOCK * core, BLOCK)

    def side(t):
        return remote(
            block_ref.at[mine, rows(1 + t)],
            block_ref.at[mine, rows(3 - 3 * t)],
            side_send.at[t],
            side_recv.at[t],
            right if t else left,
        )

    def swap(t):
        part = (pl.ds(SLAB, 2 * SLAB), pl.ds(3 * SLAB, SLAB), pl.ds(0, SLAB))[t]
        return remote(
            block_ref.at[mine, part],
            block_ref.at[mine, part],
            core_send.at[t],
            core_recv.at[t],
            sibling,
        )

    def chip(k, c):
        return (2 * lax.rem(k, 4) + c, 2 * pair + k // 4)

    barrier = pltpu.get_barrier_semaphore()
    for device in (partner, sibling, left, right):
        pl.semaphore_signal(barrier, inc=1, device_id=device, device_id_type=MESH)

    my_chip = 4 * half + z_lo
    for slab in range(2):
        target = (4 * core, 2 * pair + slab)

        @pl.when(jnp.logical_or(band != 4 * core, half != slab))
        def _():
            pl.semaphore_signal(barrier, inc=1, device_id=target, device_id_type=MESH)

    @pl.when(jnp.logical_not(jnp.logical_or(first_root, second_root)))
    def _():
        pl.semaphore_wait(barrier, 4)

    @pl.when(first_root)
    def _():
        pl.semaphore_wait(barrier, 4 + 7)
        for t in range(1, 8):
            root(0, t, chip(lax.rem(my_chip + t, 8), 0)).start()
        root_local().start()

    @pl.when(second_root)
    def _():
        pl.semaphore_wait(barrier, 4 + 8)
        for t in range(8):
            root(1, t, chip(lax.rem(my_chip + t, 8), 1)).start()

    def begin(i, carry):
        cross(i).start()
        direct(i).start()
        own(i).start()
        return carry

    lax.fori_loop(0, HALF, begin, 0)

    for slab in range(2):
        local = jnp.logical_and(first_root, half == slab)

        @pl.when(local)
        def _():
            root_local().wait()

        @pl.when(jnp.logical_not(local))
        def _():
            root_arrival(slab).wait_recv()

    for t in range(2):
        side(t).start()
    swap(0).start()

    cross(0).wait_recv()
    passed(0).start()

    side(0).wait_recv()
    swap(1).start()
    side(1).wait_recv()
    swap(2).start()
    for t in range(3):
        swap(t).wait_recv()

    lane = lax.broadcasted_iota(jnp.int32, (STRIP, CZ), 1)
    sub = lax.broadcasted_iota(jnp.int32, (STRIP, CZ), 0)

    def stencil(r, carry):
        plane, y = 4 * pair + r // (CY // STRIP), sub + STRIP * lax.rem(
            r, CY // STRIP
        )
        start = SLAB + r * STRIP
        centre = []
        for b in range(NB):
            c = block_ref[b, pl.ds(start, STRIP), :] * (-occ_ref[weight_rows[b]])
            rolled = {}
            for dz in range(-2, 3):
                if dz == 0:
                    rolled[dz] = c
                else:
                    inside = lane >= dz if dz > 0 else lane < CZ + dz
                    rolled[dz] = jnp.where(
                        inside, pltpu.roll(c, dz % CZ, axis=1), 0.0
                    )
            centre.append(rolled)
        one, nil = jnp.float32(1.0), jnp.float32(0.0)
        for dx, dy in PLANE_OFFSETS:
            there = [
                block_ref[b, pl.ds(start + dx * CY + dy, STRIP), :] for b in range(NB)
            ]
            inside_x = jnp.logical_and(plane + dx >= 0, plane + dx < 4 * PAIRS)
            for dz in range(-2, 3):
                if abs(dx) + abs(dy) + abs(dz) > 2:
                    continue
                total = centre[0][dz] * there[0]
                for b in range(1, NB):
                    total = total + centre[b][dz] * there[b]
                if dx == dy == dz == 0:
                    sides = jnp.where(plane > 0, one, nil) + jnp.where(
                        plane < 4 * PAIRS - 1, one, nil
                    )
                    count = (
                        sides
                        + jnp.where(y > 0, one, nil)
                        + jnp.where(y < CY - 1, one, nil)
                        + jnp.where(lane > 0, one, nil)
                        + jnp.where(lane < CZ - 1, one, nil)
                    )
                    factor = (36.0 + count) * (1.0 / 216.0)
                else:
                    factor = jnp.float32(coefficient((dx, dy, dz)))
                    if dx:
                        factor = jnp.where(inside_x, factor, nil)
                    if dy:
                        inside_y = y + dy >= 0 if dy < 0 else y + dy < CY
                        factor = jnp.where(inside_y, factor, nil)
                k_ref[INDEX[dx, dy, dz], pl.ds(r * STRIP, STRIP), :] = total * factor
        return carry

    lax.fori_loop(0, 4 * CY // STRIP, stencil, 0)

    def orbital(i, carry):
        @pl.when(i + 1 < HALF)
        def _():
            cross(i + 1).wait_recv()
            passed(i + 1).start()

        own(i).wait()
        direct(i).wait_recv()
        passed(i).wait_recv()

        def strip(r, inner):
            start = SLAB + r * STRIP
            sums = {}
            for dx, dy in PLANE_OFFSETS:
                there = w_ref[i, pl.ds(start + dx * CY + dy, STRIP), :]
                for dz in range(-2, 3):
                    if abs(dx) + abs(dy) + abs(dz) <= 2:
                        term = k_ref[INDEX[dx, dy, dz], pl.ds(r * STRIP, STRIP), :] * there
                        sums[dz] = term if dz not in sums else sums[dz] + term
            result = sums[0]
            for dz in (-2, -1, 1, 2):
                result = result + pltpu.roll(sums[dz], -dz % CZ, axis=1)
            out_ref[i, pl.ds(r * STRIP, STRIP), :] = result
            return inner

        lax.fori_loop(0, 4 * CY // STRIP, strip, 0)
        back(i).start()
        keep(i).start()
        return carry

    lax.fori_loop(0, HALF, orbital, 0)

    def finish(i, carry):
        cross(i).wait_send()
        direct(i).wait_send()
        passed(i).wait_send()
        keep(i).wait()
        back(i).wait()
        return carry

    lax.fori_loop(0, HALF, finish, 0)
    for t in range(2):
        side(t).wait_send()
    for t in range(3):
        swap(t).wait_send()

    @pl.when(first_root)
    def _():
        for t in range(1, 8):
            root(0, t, chip(lax.rem(my_chip + t, 8), 0)).wait_send()

    @pl.when(second_root)
    def _():
        for t in range(8):
            root(1, t, chip(lax.rem(my_chip + t, 8), 1)).wait_send()


def per_device(orbitals, occupations):
    count, planes = orbitals.shape[:2]
    groups = lax.axis_size("band")
    weight_rows = [
        s * (groups // STEPS) * count + s * BLOCK + b
        for s in range(STEPS)
        for b in range(BLOCK)
    ]
    dma = pltpu.SemaphoreType.DMA
    out = pl.pallas_call(
        functools.partial(kernel, weight_rows),
        name="exchange",
        out_shape=jax.ShapeDtypeStruct((count, planes * CY, CZ), jnp.float32),
        in_specs=[
            pl.BlockSpec(memory_space=pltpu.SMEM),
            pl.BlockSpec(memory_space=pl.ANY),
        ],
        out_specs=pl.BlockSpec(memory_space=pl.ANY),
        scratch_shapes=[
            pltpu.VMEM((HALF, 4 * SLAB, CZ), jnp.float32),
            pltpu.VMEM((NB, 4 * SLAB, CZ), jnp.float32),
            pltpu.VMEM((len(OFFSETS), 2 * SLAB, CZ), jnp.float32),
            pltpu.VMEM((HALF, 2 * SLAB, CZ), jnp.float32),
            dma((HALF,)),
            dma((HALF,)),
            dma((HALF,)),
            dma((HALF,)),
            dma((HALF,)),
            dma((HALF,)),
            dma((HALF,)),
            dma((HALF,)),
            dma((HALF,)),
            dma((HALF,)),
            dma((8,)),
            dma((2,)),
            dma,
            dma((2,)),
            dma((2,)),
            dma((3,)),
            dma((3,)),
        ],
        compiler_params=pltpu.CompilerParams(
            collective_id=0, has_side_effects=True, vmem_limit_bytes=40 * 2**20
        ),
    )(occupations, orbitals.reshape(count, planes * CY, CZ))
    return out.reshape(orbitals.shape)


def solution(mesh):
    in_specs = (P("band", "dom", None, None), P())
    out_specs = P("band", "dom", None, None)
    return jax.shard_map(
        per_device, mesh=mesh, in_specs=in_specs, out_specs=out_specs, check_vma=False
    )
```

time: 702 us -> 121 us (0.17)
  the two profiles are of different devices: /device:TPU:58 before, /device:TPU:57 now
where the time goes in v1:
time: 121 us
  Pallas kernels  118 us (98%)
  local copies, waits for them, and re-layouts  3.21 us (3%)
    pallas_call x1, Pallas kernels, per_device(): pl.pallas_call(functools.partial(kernel, weight_rows), name='exchange', o...  118 us
    unnamed x5, local copies, waits for them, and re-layouts  3.21 us

profile of v1, /device:TPU:57, one launch (start us, length us, event | category | flops | bytes accessed | tf_op | source)
XLA Modules:
  0.0 121.1 jit_solution(6178771300765580394)
XLA Ops:
  0.0 0.0 copy-start
  0.0 1.4 %copy-done = f32[12,2,128,128]{3,2,1,0:T(8,128)S(1)} copy-done((f32[12,2,128,128]{3,2,1,0:T(8,128)S(1)}, f32[12,2,128,128]{3,2,1,0:T(8,128)}, u32[]{:S(2)}) %copy-start) | copy-done | bytes 1572888
  1.4 0.0 copy-start.1
  1.4 0.7 copy-done.1
  2.1 117.8 %exchange.1 = f32[12,256,128]{2,1,0:T(8,128)S(1)} custom-call(f32[96]{0:T(128)S(1)} %copy-done.1, f32[12,256,128]{2,1,0:T(8,128)S(1)} %bitcast.3), custom_call_target="tpu_custom_call" | custom-call | tf_op jit(solution)/shard_map/exchange/pallas_call | solution.py:375
  119.9 1.1 copy.4
Async XLA Ops:
  0.0 1.4 %copy-start = (f32[12,2,128,128]{3,2,1,0:T(8,128)S(1)}, f32[12,2,128,128]{3,2,1,0:T(8,128)}, u32[]{:S(2)}) copy-start(f32[12,2,128,128]{3,2,1,0:T(8,128)} %param.2) | copy-start | bytes 4718596
  1.4 0.7 copy-start.1

commit v2 on v1

--- a/solution.py
+++ b/solution.py
@@ -17,7 +17,12 @@
 SLAB = 2 * CY
 PAIRS = 32
 HALF = 6
-STRIP = 8
+STRIP = 128
+KSTRIP = 64
+EARLY = 3
+RELAYS = (1, 2, -1, -2)
+SEEDS = (*RELAYS, 0)
+WINDOW = 3
 
 PLANE_OFFSETS = [
     (dx, dy) for dx in range(-2, 3) for dy in range(-2, 3) if abs(dx) + abs(dy) <= 2
@@ -40,9 +45,11 @@
 
 def kernel(
     weight_rows,
-    occ_ref,
+    occ_hbm,
     x_ref,
     o_ref,
+    occ_ref,
+    occ_sem,
     w_ref,
     block_ref,
     k_ref,
@@ -57,9 +64,10 @@
     back_send,
     back_recv,
     keep_sem,
-    root_send,
+    root_own,
+    seed_send,
+    relay_send,
     root_recv,
-    root_own,
     side_send,
     side_recv,
     core_send,
@@ -76,8 +84,11 @@
     left = (band, 2 * left_pair + half)
     ahead = (band, 2 * jnp.where(half == 0, right_pair, left_pair) + half)
     behind = (band, 2 * jnp.where(half == 0, left_pair, right_pair) + half)
-    first_root = band == 0
-    second_root = band == 4
+    z = 4 * half + z_lo
+
+    def chip(step, c):
+        k = lax.rem(z + step + 8, 8)
+        return (2 * lax.rem(k, 4) + c, 2 * pair + k // 4)
 
     def rows(slab):
         return pl.ds(pl.multiple_of(slab * SLAB, SLAB), SLAB)
@@ -138,128 +149,144 @@
             out_ref.at[i, rows(half)], o_ref.at[HALF * half + i], keep_sem.at[i]
         )
 
-    def root(group, t, device):
-        return remote(
-            x_ref.at[pl.ds(BLOCK * group, BLOCK)],
-            block_ref.at[pl.ds(BLOCK * group, BLOCK), rows(1 + half)],
-            root_send.at[t],
-            root_recv.at[half],
-            device,
-        )
-
-    def root_arrival(slab):
-        return remote(
-            x_ref.at[pl.ds(BLOCK * core, BLOCK)],
-            block_ref.at[pl.ds(BLOCK * core, BLOCK), rows(1 + slab)],
-            root_send.at[0],
-            root_recv.at[slab],
-            sibling,
-        )
-
-    def root_local():
+    mine = pl.ds(BLOCK * core, BLOCK)
+    is_root = jnp.logical_or(band == 0, band == 4)
+    group = band // 4
+    is_relay = jnp.logical_and(lax.rem(z, 2) == 0, lax.rem(z, 4) != 2 * core)
+    before = lax.rem(z + 6, 8) // 4
+
+    def seed(u, step):
+        return remote(
+            x_ref.at[BLOCK * group + u],
+            block_ref.at[BLOCK * group + u, rows(1 + half)],
+            seed_send.at[u, SEEDS.index(step)],
+            root_recv.at[half, u],
+            sibling if step == 0 else chip(step, group),
+        )
+
+    def seed_local(u):
         return pltpu.make_async_copy(
-            x_ref.at[pl.ds(0, BLOCK)],
-            block_ref.at[pl.ds(0, BLOCK), rows(1 + half)],
-            root_own,
-        )
-
-    mine = pl.ds(BLOCK * core, BLOCK)
-
-    def side(t):
-        return remote(
-            block_ref.at[mine, rows(1 + t)],
-            block_ref.at[mine, rows(3 - 3 * t)],
-            side_send.at[t],
-            side_recv.at[t],
-            right if t else left,
-        )
-
-    def swap(t):
-        part = (pl.ds(SLAB, 2 * SLAB), pl.ds(3 * SLAB, SLAB), pl.ds(0, SLAB))[t]
-        return remote(
-            block_ref.at[mine, part],
-            block_ref.at[mine, part],
-            core_send.at[t],
-            core_recv.at[t],
-            sibling,
-        )
-
-    def chip(k, c):
-        return (2 * lax.rem(k, 4) + c, 2 * pair + k // 4)
+            x_ref.at[u], block_ref.at[u, rows(1 + half)], root_own.at[u]
+        )
+
+    def relay(slab, u, step):
+        part = block_ref.at[BLOCK * core + u, rows(1 + slab)]
+        return remote(
+            part,
+            part,
+            relay_send.at[u, RELAYS.index(step)],
+            root_recv.at[slab, u],
+            chip(step, core),
+        )
+
+    def relays(u, act):
+        act(relay(before, u, 1))
+        if u == 0:
+            act(relay(before, u, 2))
+        act(relay(1 - before, u, -1))
+        if u == 1:
+            act(relay(1 - before, u, -2))
+
+    def arrive(u):
+        @pl.when(is_relay)
+        def _():
+            for slab in range(2):
+                relay(slab, u, 1).wait_recv()
+            relays(u, lambda copy: copy.start())
+
+        for slab in range(2):
+            local = jnp.logical_and(band == 0, half == slab)
+
+            @pl.when(local)
+            def _():
+                seed_local(u).wait()
+
+            @pl.when(jnp.logical_not(jnp.logical_or(local, is_relay)))
+            def _():
+                relay(slab, u, 1).wait_recv()
+
+    def side(slab):
+        return remote(
+            block_ref.at[mine, rows(1 + slab)],
+            block_ref.at[mine, rows(3 - 3 * slab)],
+            side_send.at[slab],
+            side_recv.at[slab],
+            (band, 2 * jnp.where(slab == 0, left_pair, right_pair) + half),
+        )
+
+    def swap(slot):
+        part = block_ref.at[mine, rows(slot)]
+        return remote(part, part, core_send.at[slot], core_recv.at[slot], sibling)
+
+    weights = pltpu.make_async_copy(occ_hbm, occ_ref, occ_sem)
+    weights.start()
 
     barrier = pltpu.get_barrier_semaphore()
-    for device in (partner, sibling, left, right):
+    near = [chip(step, c) for step in RELAYS for c in range(2)]
+    for device in (partner, sibling, left, right, *near):
         pl.semaphore_signal(barrier, inc=1, device_id=device, device_id_type=MESH)
-
-    my_chip = 4 * half + z_lo
+    pl.semaphore_wait(barrier, 4 + len(near))
+
+    @pl.when(band == 0)
+    def _():
+        for u in range(BLOCK):
+            seed_local(u).start()
+
+    @pl.when(band == 4)
+    def _():
+        for u in range(BLOCK):
+            seed(u, 0).start()
+
+    @pl.when(is_root)
+    def _():
+        for steps in ((2, -2), (1, -1)):
+            for u in range(BLOCK):
+                for step in steps:
+                    seed(u, step).start()
+
+    for i in range(EARLY):
+        direct(i).start()
+    for i in range(HALF):
+        own(i).start()
+
+    def advance(i):
+        cross(i).wait_recv()
+        passed(i).start()
+
+        @pl.when(i + WINDOW < HALF)
+        def _():
+            cross(i + WINDOW).start()
+
+        @pl.when(i + EARLY < HALF)
+        def _():
+            direct(i + EARLY).start()
+
+    for u in range(BLOCK):
+        arrive(u)
     for slab in range(2):
-        target = (4 * core, 2 * pair + slab)
-
-        @pl.when(jnp.logical_or(band != 4 * core, half != slab))
-        def _():
-            pl.semaphore_signal(barrier, inc=1, device_id=target, device_id_type=MESH)
-
-    @pl.when(jnp.logical_not(jnp.logical_or(first_root, second_root)))
-    def _():
-        pl.semaphore_wait(barrier, 4)
-
-    @pl.when(first_root)
-    def _():
-        pl.semaphore_wait(barrier, 4 + 7)
-        for t in range(1, 8):
-            root(0, t, chip(lax.rem(my_chip + t, 8), 0)).start()
-        root_local().start()
-
-    @pl.when(second_root)
-    def _():
-        pl.semaphore_wait(barrier, 4 + 8)
-        for t in range(8):
-            root(1, t, chip(lax.rem(my_chip + t, 8), 1)).start()
-
-    def begin(i, carry):
+        side(slab).start()
+        swap(1 + slab).start()
+    for i in range(WINDOW):
         cross(i).start()
-        direct(i).start()
-        own(i).start()
-        return carry
-
-    lax.fori_loop(0, HALF, begin, 0)
-
+    advance(0)
     for slab in range(2):
-        local = jnp.logical_and(first_root, half == slab)
-
-        @pl.when(local)
-        def _():
-            root_local().wait()
-
-        @pl.when(jnp.logical_not(local))
-        def _():
-            root_arrival(slab).wait_recv()
-
-    for t in range(2):
-        side(t).start()
-    swap(0).start()
-
-    cross(0).wait_recv()
-    passed(0).start()
-
-    side(0).wait_recv()
-    swap(1).start()
-    side(1).wait_recv()
-    swap(2).start()
-    for t in range(3):
-        swap(t).wait_recv()
-
-    lane = lax.broadcasted_iota(jnp.int32, (STRIP, CZ), 1)
-    sub = lax.broadcasted_iota(jnp.int32, (STRIP, CZ), 0)
+        side(slab).wait_recv()
+        swap(3 - 3 * slab).start()
+    for slot in range(4):
+        swap(slot).wait_recv()
+
+    weights.wait()
+    lane = lax.broadcasted_iota(jnp.int32, (KSTRIP, CZ), 1)
+    sub = lax.broadcasted_iota(jnp.int32, (KSTRIP, CZ), 0)
 
     def stencil(r, carry):
-        plane, y = 4 * pair + r // (CY // STRIP), sub + STRIP * lax.rem(
-            r, CY // STRIP
-        )
-        start = SLAB + r * STRIP
+        plane, y = 4 * pair + r // (CY // KSTRIP), sub + KSTRIP * lax.rem(
+            r, CY // KSTRIP
+        )
+        start = SLAB + r * KSTRIP
         centre = []
         for b in range(NB):
-            c = block_ref[b, pl.ds(start, STRIP), :] * (-occ_ref[weight_rows[b]])
+            c = block_ref[b, pl.ds(start, KSTRIP), :] * (-occ_ref[weight_rows[b]])
             rolled = {}
             for dz in range(-2, 3):
                 if dz == 0:
@@ -273,7 +300,7 @@
         one, nil = jnp.float32(1.0), jnp.float32(0.0)
         for dx, dy in PLANE_OFFSETS:
             there = [
-                block_ref[b, pl.ds(start + dx * CY + dy, STRIP), :] for b in range(NB)
+                block_ref[b, pl.ds(start + dx * CY + dy, KSTRIP), :] for b in range(NB)
             ]
             inside_x = jnp.logical_and(plane + dx >= 0, plane + dx < 4 * PAIRS)
             for dz in range(-2, 3):
@@ -301,16 +328,15 @@
                     if dy:
                         inside_y = y + dy >= 0 if dy < 0 else y + dy < CY
                         factor = jnp.where(inside_y, factor, nil)
-                k_ref[INDEX[dx, dy, dz], pl.ds(r * STRIP, STRIP), :] = total * factor
+                k_ref[INDEX[dx, dy, dz], pl.ds(r * KSTRIP, KSTRIP), :] = total * factor
         return carry
 
-    lax.fori_loop(0, 4 * CY // STRIP, stencil, 0)
+    lax.fori_loop(0, 4 * CY // KSTRIP, stencil, 0)
 
     def orbital(i, carry):
         @pl.when(i + 1 < HALF)
         def _():
-            cross(i + 1).wait_recv()
-            passed(i + 1).start()
+            advance(i + 1)
 
         own(i).wait()
         direct(i).wait_recv()
@@ -331,8 +357,13 @@
             out_ref[i, pl.ds(r * STRIP, STRIP), :] = result
             return inner
 
-        lax.fori_loop(0, 4 * CY // STRIP, strip, 0)
+        def planes(slab):
+            first = slab * (SLAB // STRIP)
+            lax.fori_loop(first, first + SLAB // STRIP, strip, 0)
+
+        planes(1 - half)
         back(i).start()
+        planes(half)
         keep(i).start()
         return carry
 
@@ -347,20 +378,26 @@
         return carry
 
     lax.fori_loop(0, HALF, finish, 0)
-    for t in range(2):
-        side(t).wait_send()
-    for t in range(3):
-        swap(t).wait_send()
-
-    @pl.when(first_root)
-    def _():
-        for t in range(1, 8):
-            root(0, t, chip(lax.rem(my_chip + t, 8), 0)).wait_send()
-
-    @pl.when(second_root)
-    def _():
-        for t in range(8):
-            root(1, t, chip(lax.rem(my_chip + t, 8), 1)).wait_send()
+    for slab in range(2):
+        side(slab).wait_send()
+    for slot in range(4):
+        swap(slot).wait_send()
+
+    @pl.when(is_relay)
+    def _():
+        for u in range(BLOCK):
+            relays(u, lambda copy: copy.wait_send())
+
+    @pl.when(band == 4)
+    def _():
+        for u in range(BLOCK):
+            seed(u, 0).wait_send()
+
+    @pl.when(is_root)
+    def _():
+        for u in range(BLOCK):
+            for step in RELAYS:
+                seed(u, step).wait_send()
 
 
 def per_device(orbitals, occupations):
@@ -377,11 +414,13 @@
         name="exchange",
         out_shape=jax.ShapeDtypeStruct((count, planes * CY, CZ), jnp.float32),
         in_specs=[
-            pl.BlockSpec(memory_space=pltpu.SMEM),
-            pl.BlockSpec(memory_space=pl.ANY),
+            pl.BlockSpec(memory_space=pltpu.HBM),
+            pl.BlockSpec(memory_space=pltpu.HBM),
         ],
         out_specs=pl.BlockSpec(memory_space=pl.ANY),
         scratch_shapes=[
+            pltpu.SMEM(occupations.shape, jnp.float32),
+            dma,
             pltpu.VMEM((HALF, 4 * SLAB, CZ), jnp.float32),
             pltpu.VMEM((NB, 4 * SLAB, CZ), jnp.float32),
             pltpu.VMEM((len(OFFSETS), 2 * SLAB, CZ), jnp.float32),
@@ -396,13 +435,14 @@
             dma((HALF,)),
             dma((HALF,)),
             dma((HALF,)),
-            dma((8,)),
-            dma((2,)),
-            dma,
+            dma((BLOCK,)),
+            dma((BLOCK, len(SEEDS))),
+            dma((BLOCK, len(RELAYS))),
+            dma((2, BLOCK)),
             dma((2,)),
             dma((2,)),
-            dma((3,)),
-            dma((3,)),
+            dma((4,)),
+            dma((4,)),
         ],
         compiler_params=pltpu.CompilerParams(
             collective_id=0, has_side_effects=True, vmem_limit_bytes=40 * 2**20

time: 121 us -> 98.9 us (0.82)
  the two profiles are of different devices: /device:TPU:57 before, /device:TPU:65 now
where the time goes in v2:
time: 98.9 us; the launch traced here: 98.7 us
  Pallas kernels  95.5 us (97%)
  local copies, waits for them, and re-layouts  3.21 us (3%)
    pallas_call x1, Pallas kernels, per_device(): pl.pallas_call(functools.partial(kernel, weight_rows), name='exchange', o...  95.5 us
    unnamed x5, local copies, waits for them, and re-layouts  3.21 us

profile of v2, /device:TPU:65, one launch (start us, length us, event | category | flops | bytes accessed | tf_op | source)
XLA Modules:
  0.0 98.7 jit_solution(12104785899812548682)
XLA Ops:
  0.0 0.0 copy-start
  0.0 1.4 %copy-done = f32[12,2,128,128]{3,2,1,0:T(8,128)S(1)} copy-done((f32[12,2,128,128]{3,2,1,0:T(8,128)S(1)}, f32[12,2,128,128]{3,2,1,0:T(8,128)}, u32[]{:S(2)}) %copy-start) | copy-done | bytes 1572888
  1.4 0.0 copy-start.1
  1.4 0.7 copy-done.1
  2.1 95.5 %exchange.1 = f32[12,256,128]{2,1,0:T(8,128)S(1)} custom-call(f32[96]{0:T(128)S(1)} %copy-done.1, f32[12,256,128]{2,1,0:T(8,128)S(1)} %bitcast.3), custom_call_target="tpu_custom_call" | custom-call | tf_op jit(solution)/shard_map/exchange/pallas_call | solution.py:412
  97.6 1.1 %copy.4 = f32[12,2,128,128]{3,2,1,0:T(8,128)} copy(f32[12,2,128,128]{3,2,1,0:T(8,128)S(1)} %bitcast.2) | data formatting | bytes 3145728
Async XLA Ops:
  0.0 1.4 %copy-start = (f32[12,2,128,128]{3,2,1,0:T(8,128)S(1)}, f32[12,2,128,128]{3,2,1,0:T(8,128)}, u32[]{:S(2)}) copy-start(f32[12,2,128,128]{3,2,1,0:T(8,128)} %param.2) | copy-start | bytes 4718596
  1.4 0.7 copy-start.1

commit v3 on v2

--- a/solution.py
+++ b/solution.py
@@ -180,12 +180,12 @@
         )
 
     def relays(u, act):
-        act(relay(before, u, 1))
         if u == 0:
             act(relay(before, u, 2))
+        else:
+            act(relay(1 - before, u, -2))
         act(relay(1 - before, u, -1))
-        if u == 1:
-            act(relay(1 - before, u, -2))
+        act(relay(before, u, 1))
 
     def arrive(u):
         @pl.when(is_relay)
@@ -447,7 +447,12 @@
         compiler_params=pltpu.CompilerParams(
             collective_id=0, has_side_effects=True, vmem_limit_bytes=40 * 2**20
         ),
-    )(occupations, orbitals.reshape(count, planes * CY, CZ))
+    )(
+        pltpu.with_memory_space_constraint(occupations, pltpu.HBM),
+        pltpu.with_memory_space_constraint(
+            orbitals.reshape(count, planes * CY, CZ), pltpu.HBM
+        ),
+    )
     return out.reshape(orbitals.shape)
 
 

time: 98.9 us -> 95.2 us (0.963)
  the two profiles are of different devices: /device:TPU:65 before, /device:TPU:159 now
where the time goes in v3:
time: 95.2 us; the launch traced here: 95.1 us
  Pallas kernels  93.9 us (99%)
  local copies, waits for them, and re-layouts  1.15 us (1%)
    pallas_call x1, Pallas kernels, per_device(): pl.pallas_call(functools.partial(kernel, weight_rows), name='exchange', o...  93.9 us

profile of v3, /device:TPU:159, one launch (start us, length us, event | category | flops | bytes accessed | tf_op | source)
XLA Modules:
  0.0 95.1 jit_solution(7120634854510470085)
XLA Ops:
  0.0 93.9 %exchange.1 = f32[12,256,128]{2,1,0:T(8,128)S(1)} custom-call(f32[96]{0:T(128)} %occ_hbm.1, f32[12,256,128]{2,1,0:T(8,128)} %bitcast.3), custom_call_target="tpu_custom_call" | custom-call | tf_op jit(solution)/shard_map/exchange/pallas_call | solution.py:412
  93.9 1.1 %copy.4 = f32[12,2,128,128]{3,2,1,0:T(8,128)} copy(f32[12,2,128,128]{3,2,1,0:T(8,128)S(1)} %bitcast.2) | data formatting | bytes 3145728

commit v4 on v3

--- a/solution.py
+++ b/solution.py
@@ -261,12 +261,25 @@
         def _():
             direct(i + EARLY).start()
 
-    for u in range(BLOCK):
-        arrive(u)
+    at_root = lax.rem(z, 4) == 2 * core
+    arrive(0)
+
+    @pl.when(at_root)
+    def _():
+        for i in range(3):
+            cross(i).start()
+
+    arrive(1)
     for slab in range(2):
         side(slab).start()
         swap(1 + slab).start()
-    for i in range(WINDOW):
+
+    @pl.when(jnp.logical_not(at_root))
+    def _():
+        for i in range(3):
+            cross(i).start()
+
+    for i in range(3, WINDOW):
         cross(i).start()
     advance(0)
     for slab in range(2):

time: 95.2 us -> 95.1 us (level)
  the two profiles are of different devices: /device:TPU:159 before, /device:TPU:192 now
where the time goes in v4:
time: 95.1 us; the launch traced here: 95 us
  Pallas kernels  93.8 us (99%)
  local copies, waits for them, and re-layouts  1.15 us (1%)
    pallas_call x1, Pallas kernels, per_device(): pl.pallas_call(functools.partial(kernel, weight_rows), name='exchange', o...  93.8 us

profile of v4, /device:TPU:192, one launch (start us, length us, event | category | flops | bytes accessed | tf_op | source)
XLA Modules:
  0.0 95.0 jit_solution(5817738044814631354)
XLA Ops:
  0.0 93.8 %exchange.1 = f32[12,256,128]{2,1,0:T(8,128)S(1)} custom-call(f32[96]{0:T(128)} %occ_hbm.1, f32[12,256,128]{2,1,0:T(8,128)} %bitcast.3), custom_call_target="tpu_custom_call" | custom-call | tf_op jit(solution)/shard_map/exchange/pallas_call | solution.py:425
  93.8 1.1 %copy.4 = f32[12,2,128,128]{3,2,1,0:T(8,128)} copy(f32[12,2,128,128]{3,2,1,0:T(8,128)S(1)} %bitcast.2) | data formatting | bytes 3145728
